TPU v7x, 256 devices: a whole 4x4x8 slice. The times are simulated.
256 devices in a mesh: inst: 4 (over y_lo, core), cell: 64 (over z, y_hi, x).
Axes of the slice: x: 4, y: 4 (y_hi: 2, y_lo: 2; y = y_hi * 2 + y_lo), z: 8, core: 2. Of those that a mesh axis runs over, the one named last changes fastest.
Arguments:
- state: float32 [8, 6, 128, 2048], P('inst', None, 'cell'), may hold values from -0.8 to 5, as said below
- pseudo_rate: float32 [128, 2048], P('cell'), may hold values from 0.001 to 0.01
- line_next: int32 [2048], replicated, may hold values from 0 to 2047, each once
- face_codes: int32 [2, 64], replicated, may hold values from 0 to 2
Outputs:
- new_state: float32 [8, 6, 128, 2048], P('inst', None, 'cell')
Inputs may be any that keep to these rules, and one draw needn't show every extreme that they name: `state`: conserved variables of a gas with ratio of specific heats 1.4: in every cell density lies between 0.7 and 1.3 and pressure between 0.6 and 1.4. `line_next`: every line is named once. `face_codes`: 0 a slip wall, 1 a fixed inflow state, 2 extrapolation.
All inputs are finite; a program needn't handle non-finite values.
Results may differ from a plain program's by a relative error of at most 0.0003.
Values sent between devices are 32-bit elements; how exact they have to be, the bound alone decides.
A program may use at most 64 MiB of HBM per device.

v0:
```python
import jax
import jax.numpy as jnp
import numpy as np
from jax import lax
from jax.experimental import pallas as pl
from jax.experimental.pallas import tpu as pltpu
from jax.sharding import PartitionSpec as P

NT = 8
CELLS = 64
CHUNKS = 16
LANES = 128
TILE_LINES = 32
GAMMA_GAS = 1.4
FREE_STATE = (1.0, 0.5, 0.0, 0.0, 2.625, 0.2)
F32 = jnp.float32
FACTOR_PLANES = 168


def spectral_table():
    offsets = np.arange(NT)[:, None] - np.arange(NT)[None, :]
    angles = np.pi * offsets / NT
    safe_sin = np.where(offsets == 0, 1.0, np.sin(angles))
    parity = np.where(np.mod(offsets, 2) == 0, -1.0, 1.0)
    return np.where(offsets == 0, 0.0, 0.5 * parity * np.cos(angles) / safe_sin)


def time_weight(inst, row, slot, column):
    table = spectral_table()
    values = [float(table[2 * i + row, 2 * (i ^ slot) + column]) for i in range(NT // 2)]
    weight = jnp.float32(values[3])
    for i in (2, 1, 0):
        weight = jnp.where(inst == i, jnp.float32(values[i]), weight)
    return weight


def primitives(cell):
    inverse = 1.0 / cell[0]
    vel_x = cell[1] * inverse
    vel_y = cell[2] * inverse
    vel_z = cell[3] * inverse
    pressure = 0.4 * (cell[4] - 0.5 * cell[0] * (vel_x * vel_x + vel_y * vel_y + vel_z * vel_z))
    sound = jnp.sqrt(GAMMA_GAS * pressure * inverse)
    return vel_x, vel_y, pressure, sound


def flux(cell, velocity, pressure, component):
    rows = [cell[v] * velocity for v in range(6)]
    rows[component] = rows[component] + pressure
    rows[4] = rows[4] + pressure * velocity
    return rows


def line_part(cells):
    parts = [primitives(c) for c in cells]
    pressure = [q[2] for q in parts]
    radius = [jnp.abs(q[0]) + q[3] for q in parts]
    fluxes = [flux(cells[j], parts[j][0], pressure[j], 1) for j in range(1, 5)]
    sensor = [
        jnp.abs(pressure[j + 1] - 2.0 * pressure[j] + pressure[j - 1])
        / (pressure[j + 1] + 2.0 * pressure[j] + pressure[j - 1])
        for j in range(1, 5)
    ]
    faces = []
    for j in range(1, 4):
        second = 0.25 * jnp.maximum(sensor[j - 1], sensor[j])
        fourth = jnp.maximum(0.0, 0.03125 - second)
        face_radius = 0.5 * (radius[j] + radius[j + 1])
        rows = []
        for v in range(6):
            near = cells[j + 1][v] - cells[j][v]
            far = cells[j + 2][v] - cells[j - 1][v] - 3.0 * near
            rows.append(
                0.5 * (fluxes[j - 1][v] + fluxes[j][v])
                - face_radius * (second * near - fourth * far)
            )
        faces.append(rows)
    return [[faces[c + 1][v] - faces[c][v] for v in range(6)] for c in range(2)]


def ghost_cells(near, far, codes):
    inflow = [jnp.full(codes.shape, FREE_STATE[v], F32) for v in range(6)]

    def pick(mirror, v):
        reflected = -mirror[v] if v == 1 else mirror[v]
        return jnp.where(codes == 0, reflected, jnp.where(codes == 1, inflow[v], near[v]))

    return [pick(near, v) for v in range(6)], [pick(far, v) for v in range(6)]


def mat_mat(a, b):
    return (
        a[0] * b[0] + a[1] * b[2],
        a[0] * b[1] + a[1] * b[3],
        a[2] * b[0] + a[3] * b[2],
        a[2] * b[1] + a[3] * b[3],
    )


def mat_vec(a, x):
    return (a[0] * x[0] + a[1] * x[1], a[2] * x[0] + a[3] * x[1])


def mat_inv(m):
    reciprocal = 1.0 / (m[0] * m[3] - m[1] * m[2])
    return (m[3] * reciprocal, -m[1] * reciprocal, -m[2] * reciprocal, m[0] * reciprocal)


def plus(a, b):
    return tuple(x + y for x, y in zip(a, b))


def minus(a):
    return tuple(-x for x in a)


def rolled(members, shift, axis):
    return tuple(pltpu.roll(m, shift % 8, axis) for m in members)


STEPS = (
    (0, 1, 2, False),
    (2, 3, 4, False),
    (4, 5, 6, False),
    (6, 7, 0, True),
    (1, 3, 5, False),
    (5, 7, 1, True),
    (3, 7, 3, True),
)
BEFORE = {0: (7, True), 2: (1, False), 4: (3, False), 6: (5, False), 1: (7, True), 5: (3, False), 3: (7, True)}
AFTER = {0: 1, 2: 3, 4: 5, 6: 7, 1: 3, 5: 7, 3: 7}


def factorise(coef_ref, fac_ref):
    def rows(kind, v):
        return coef_ref[kind, 8 * v : 8 * v + 8, :]

    plane = lax.broadcasted_iota(jnp.int32, (8, LANES), 0)
    low = [rows(0, v) for v in range(8)]
    high = [rows(1, v) for v in range(8)]
    before = [jnp.where(plane == 0, 0.0, pltpu.roll(high[7], 1, 0))] + high[:7]
    after = low[1:] + [jnp.where(plane == 7, 0.0, pltpu.roll(low[0], 7, 0))]
    zero = jnp.zeros((8, LANES), F32)
    sub, diag, sup = {}, {}, {}
    for v in range(8):
        a, b, c, d = before[v], low[v], high[v], after[v]
        mid_low = rows(2, v) * b + 0.5 * (a + 2.0 * b + c) + 0.25 * (a + 4.0 * b + c)
        mid_high = rows(3, v) * c + 0.5 * (b + 2.0 * c + d) + 0.25 * (b + 4.0 * c + d)
        sub[v] = (0.25 * a, -(a + b), zero, 0.25 * b)
        diag[v] = (mid_low, -(b + c), -(b + c), mid_high)
        sup[v] = (0.25 * c, zero, -(c + d), 0.25 * d)
    sub[0] = tuple(jnp.where(plane == 0, 0.0, m) for m in sub[0])
    sup[7] = tuple(jnp.where(plane == 7, 0.0, m) for m in sup[7])
    count = [0]

    def keep(members):
        for m in members:
            fac_ref[count[0]] = m
            count[0] += 1

    inverse = {}
    for e, o, n, wraps in STEPS:
        for x in (e, n):
            if x not in inverse:
                inverse[x] = mat_inv(diag[x])
        inv_n, sub_n, sup_n = inverse[n], sub[n], sup[n]
        if wraps:
            inv_n, sub_n, sup_n = rolled(inv_n, -1, 0), rolled(sub_n, -1, 0), rolled(sup_n, -1, 0)
        left = minus(mat_mat(sub[o], inverse[e]))
        right = minus(mat_mat(sup[o], inv_n))
        keep(left)
        keep(right)
        keep(inverse[e])
        keep(mat_mat(inverse[e], sub[e]))
        keep(mat_mat(inverse[e], sup[e]))
        sub[o] = mat_mat(left, sub[e])
        diag[o] = plus(diag[o], plus(mat_mat(left, sup[e]), mat_mat(right, sub_n)))
        sup[o] = mat_mat(right, sup_n)
    s, d, u = sub[7], diag[7], sup[7]
    for h in (1, 2, 4):
        inv = mat_inv(d)
        left = minus(mat_mat(s, rolled(inv, h, 0)))
        right = minus(mat_mat(u, rolled(inv, -h, 0)))
        keep(left)
        keep(right)
        s_low, u_low = rolled(s, h, 0), rolled(u, h, 0)
        s_high, u_high = rolled(s, -h, 0), rolled(u, -h, 0)
        d = plus(d, plus(mat_mat(left, u_low), mat_mat(right, s_high)))
        s, u = mat_mat(left, s_low), mat_mat(right, u_high)
    keep(mat_inv(d))


def substitute(fac_ref, side_ref, out_ref):
    def fac(first):
        return tuple(fac_ref[first + j][None] for j in range(4))

    r = [
        tuple(side_ref[:, c, 8 * v : 8 * v + 8, :] for c in range(2)) for v in range(8)
    ]
    at = 0
    bases = {}
    for e, o, n, wraps in STEPS:
        side_n = rolled(r[n], -1, 1) if wraps else r[n]
        r[o] = plus(r[o], plus(mat_vec(fac(at), r[e]), mat_vec(fac(at + 4), side_n)))
        bases[e] = at + 8
        at += 20
    x = r[7]
    for h in (1, 2, 4):
        x = plus(
            x,
            plus(mat_vec(fac(at), rolled(x, h, 1)), mat_vec(fac(at + 4), rolled(x, -h, 1))),
        )
        at += 8
    values = {7: mat_vec(fac(at), x)}
    for e in (3, 5, 1, 6, 4, 2, 0):
        base = bases[e]
        prior, wraps = BEFORE[e]
        low = rolled(values[prior], 1, 1) if wraps else values[prior]
        back = plus(mat_vec(fac(base + 4), low), mat_vec(fac(base + 8), values[AFTER[e]]))
        values[e] = tuple(a - b for a, b in zip(mat_vec(fac(base), r[e]), back))
    for v in range(8):
        for c in range(2):
            out_ref[:, c, 8 * v : 8 * v + 8, :] = values[v][c]


def invert_lines(next_ref, prev_ref):
    lane = lax.broadcasted_iota(jnp.int32, (CHUNKS, LANES), 1).astype(F32)
    chunk = lax.broadcasted_iota(jnp.int32, (CHUNKS, LANES), 0)
    slot = lax.broadcasted_iota(jnp.int32, (LANES, LANES), 0)

    def body(q, total):
        row = next_ref[pl.ds(q, 1), :]
        hit = jnp.broadcast_to(row >> 7, (CHUNKS, LANES)) == chunk
        place = jnp.where(jnp.broadcast_to(row & 127, (LANES, LANES)) == slot, 1.0, 0.0)
        left = jnp.concatenate([jnp.where(hit, lane, 0.0), jnp.where(hit, 1.0, 0.0)], axis=0)
        found = lax.dot_general(
            left.astype(jnp.bfloat16),
            place.astype(jnp.bfloat16),
            (((1,), (1,)), ((), ())),
            preferred_element_type=F32,
        )
        return total + found[:CHUNKS] + found[CHUNKS:] * (q.astype(F32) * 128.0)

    total = lax.fori_loop(0, CHUNKS, body, jnp.zeros((CHUNKS, LANES), F32))
    prev_ref[...] = total.astype(jnp.int32)


def gather_lines(source, target, index_ref):
    source_rows = source.reshape(24 * CHUNKS, LANES)
    target_rows = target.reshape(24 * CHUNKS, LANES)

    def body(c, carry):
        row = jnp.broadcast_to(index_ref[pl.ds(c, 1), :], (8, LANES))
        lane = row & 127
        chunk = row >> 7
        found = [jnp.zeros((8, LANES), F32) for _ in range(3)]
        for s in range(CHUNKS):
            hit = chunk == s
            for g in range(3):
                rows = source_rows[pl.ds(g * 8 * CHUNKS + s, 8, stride=CHUNKS), :]
                found[g] = jnp.where(hit, jnp.take_along_axis(rows, lane, axis=1), found[g])
        for g in range(3):
            target_rows[pl.ds(g * 8 * CHUNKS + c, 8, stride=CHUNKS), :] = found[g]
        return carry

    lax.fori_loop(0, CHUNKS, body, 0)


def kernel(
    state_ref, rate_ref, next_ref, codes_ref, out_ref,
    own, low, high, other, shifted, kflux, kprev, rhs, lp, prev, codes, coef, fac, side, delta,
    load_sem, ghost_sem, inst_sem, coef_sem, side_sem, back_sem, self_sem,
):
    me = lax.axis_index("cell")
    inst = lax.axis_index("inst")
    barrier = pltpu.get_barrier_semaphore()

    def greet(j, carry):
        pl.semaphore_signal(barrier, 1, device_id={"cell": lax.rem(me + j, CELLS)})
        return carry

    lax.fori_loop(1, CELLS, greet, 0)
    for j in range(1, 4):
        pl.semaphore_signal(barrier, 1, device_id={"inst": inst ^ j})

    loads = [
        pltpu.make_async_copy(state_ref.at[:, :, :, c], own.at[:, :, c], load_sem.at[c])
        for c in range(2)
    ] + [
        pltpu.make_async_copy(rate_ref.at[:, c], lp.at[i, 2 + c], load_sem.at[2 + 2 * i + c])
        for i in range(2)
        for c in range(2)
    ]
    for copy in loads:
        copy.start()
    invert_lines(next_ref, prev)
    codes[...] = jnp.zeros((8, LANES), jnp.int32)
    codes[0:2, 0:64] = codes_ref[...]
    for copy in loads:
        copy.wait()

    def own_radius(i, carry):
        for c in range(2):
            vel_x, _, _, sound = primitives([own[i, v, c] for v in range(6)])
            lp[i, c] = jnp.abs(vel_x) + sound
        return carry

    lax.fori_loop(0, 2, own_radius, 0)
    gather_lines(own, shifted, next_ref)

    pl.semaphore_wait(barrier, CELLS - 1 + 3)

    right = lax.rem(me + 1, CELLS)
    left = lax.rem(me + CELLS - 1, CELLS)
    to_pair = pltpu.make_async_remote_copy(
        own, other.at[1], inst_sem.at[0], inst_sem.at[1], device_id={"inst": inst ^ 2}
    )
    to_pair.start()
    to_right = pltpu.make_async_remote_copy(
        own, low, ghost_sem.at[0], ghost_sem.at[1], device_id={"cell": right}
    )
    to_right.start()
    to_left = pltpu.make_async_remote_copy(
        own, high, ghost_sem.at[2], ghost_sem.at[3], device_id={"cell": left}
    )
    to_left.start()
    to_twin = pltpu.make_async_remote_copy(
        own, other.at[0], inst_sem.at[2], inst_sem.at[3], device_id={"inst": inst ^ 1}
    )
    to_twin.start()

    my_row = (me & 7) * 8 + (me >> 3)

    def send_coef(j, carry):
        peer = lax.rem(me + j, CELLS)
        pltpu.make_async_remote_copy(
            lp.at[peer >> 5, :, peer & 15],
            coef.at[:, my_row],
            coef_sem.at[0],
            coef_sem.at[1],
            device_id={"cell": peer},
        ).start()
        return carry

    lax.fori_loop(1, CELLS, send_coef, 0)
    my_coef = pltpu.make_async_copy(lp.at[me >> 5, :, me & 15], coef.at[:, my_row], self_sem.at[0])
    my_coef.start()

    def pitch_flux(i, carry):
        for c in range(2):
            here = [own[i, v, c] for v in range(6)]
            there = [shifted[i, v, c] for v in range(6)]
            _, vel_h, p_h, sound_h = primitives(here)
            _, vel_t, p_t, sound_t = primitives(there)
            flux_h = flux(here, vel_h, p_h, 2)
            flux_t = flux(there, vel_t, p_t, 2)
            radius = 0.25 * (jnp.abs(vel_h) + sound_h + jnp.abs(vel_t) + sound_t)
            for v in range(6):
                kflux[i, v, c] = 0.5 * (flux_h[v] + flux_t[v]) - radius * (there[v] - here[v])
        return carry

    lax.fori_loop(0, 2, pitch_flux, 0)
    gather_lines(kflux, kprev, prev)

    to_pair.wait_recv()
    to_forward = pltpu.make_async_remote_copy(
        other.at[1], other.at[2], inst_sem.at[4], inst_sem.at[5], device_id={"inst": inst ^ 1}
    )
    to_forward.start()

    pltpu.make_async_copy(
        coef.at[:, pl.ds(0, CELLS - 1)], coef.at[:, pl.ds(0, CELLS - 1)], coef_sem.at[1]
    ).wait()
    my_coef.wait()
    factorise(coef, fac)

    to_right.wait_recv()
    to_left.wait_recv()
    spread = lax.broadcasted_iota(jnp.int32, (CHUNKS, LANES), 0) * 4 + (
        lax.broadcasted_iota(jnp.int32, (CHUNKS, LANES), 1) // TILE_LINES
    )
    end_codes = [
        jnp.take_along_axis(jnp.broadcast_to(codes[e : e + 1, :], (CHUNKS, LANES)), spread, axis=1)
        for e in range(2)
    ]
    first = me == 0
    last = me == CELLS - 1

    def add_line(i, carry):
        mine = [[own[i, v, c] for v in range(6)] for c in range(2)]
        low_near, low_far = ghost_cells(mine[0], mine[1], end_codes[0])
        high_near, high_far = ghost_cells(mine[1], mine[0], end_codes[1])
        cells = [
            [jnp.where(first, low_far[v], low[i, v, 0]) for v in range(6)],
            [jnp.where(first, low_near[v], low[i, v, 1]) for v in range(6)],
            mine[0],
            mine[1],
            [jnp.where(last, high_near[v], high[i, v, 0]) for v in range(6)],
            [jnp.where(last, high_far[v], high[i, v, 1]) for v in range(6)],
        ]
        parts = line_part(cells)
        for c in range(2):
            for v in range(6):
                rhs[i, v, c] = kprev[i, v, c] - kflux[i, v, c] - parts[c][v]
        return carry

    lax.fori_loop(0, 2, add_line, 0)
    to_twin.wait_recv()
    to_forward.wait_recv()
    weights = [
        [[time_weight(inst, n, slot, m) for m in range(2)] for slot in range(4)] for n in range(2)
    ]

    def add_time(v, carry):
        for c in range(2):
            planes = [[own[m, v, c] for m in range(2)]] + [
                [other[slot, m, v, c] for m in range(2)] for slot in range(3)
            ]
            for n in range(2):
                total = rhs[n, v, c]
                for slot in range(4):
                    for m in range(2):
                        if slot == 0 and m == n:
                            continue
                        total = total - weights[n][slot][m] * planes[slot][m]
                rhs[n, v, c] = total
        return carry

    lax.fori_loop(0, 6, add_time, 0)

    def send_side(j, carry):
        peer = lax.rem(me + j, CELLS)
        pltpu.make_async_remote_copy(
            rhs.at[peer >> 5, pl.ds(((peer >> 4) & 1) * 3, 3), :, peer & 15],
            side.at[:, :, my_row],
            side_sem.at[0],
            side_sem.at[1],
            device_id={"cell": peer},
        ).start()
        return carry

    lax.fori_loop(1, CELLS, send_side, 0)
    my_inst, my_var, my_chunk = me >> 5, ((me >> 4) & 1) * 3, me & 15
    my_side = pltpu.make_async_copy(
        rhs.at[my_inst, pl.ds(my_var, 3), :, my_chunk], side.at[:, :, my_row], self_sem.at[1]
    )
    my_side.start()
    many = side.at[:, :, pl.ds(0, CELLS - 1)]
    pltpu.make_async_copy(many, many, side_sem.at[1]).wait()
    my_side.wait()
    substitute(fac, side, delta)

    def send_back(j, carry):
        peer = lax.rem(me + j, CELLS)
        pltpu.make_async_remote_copy(
            delta.at[:, :, (peer & 7) * 8 + (peer >> 3)],
            out_ref.at[my_inst, pl.ds(my_var, 3), my_chunk],
            back_sem.at[0],
            back_sem.at[1],
            device_id={"cell": peer},
        ).start()
        return carry

    lax.fori_loop(1, CELLS, send_back, 0)
    my_back = pltpu.make_async_copy(
        delta.at[:, :, my_row], out_ref.at[my_inst, pl.ds(my_var, 3), my_chunk], self_sem.at[2]
    )
    my_back.start()
    for copy in (to_pair, to_right, to_left, to_twin, to_forward):
        copy.wait_send()
    few = coef.at[:, pl.ds(0, CELLS - 1)]
    pltpu.make_async_copy(few, few, coef_sem.at[0]).wait()
    pltpu.make_async_copy(many, many, side_sem.at[0]).wait()
    pltpu.make_async_copy(many, many, back_sem.at[0]).wait()
    pltpu.make_async_copy(many, many, back_sem.at[1]).wait()
    my_back.wait()


def local(state, pseudo_rate, line_next, face_codes):
    view = state.reshape(2, 6, 2, CHUNKS, LANES).transpose(0, 1, 3, 2, 4)
    rate = pseudo_rate.reshape(2, CHUNKS, LANES).transpose(1, 0, 2)
    block = (2, 6, 2, CHUNKS, LANES)
    in_vmem = pl.BlockSpec(memory_space=pltpu.VMEM)
    in_place = pl.BlockSpec(memory_space=pl.ANY)
    dma = pltpu.SemaphoreType.DMA
    update = pl.pallas_call(
        kernel,
        out_shape=jax.ShapeDtypeStruct((2, 6, CHUNKS, 2, LANES), F32),
        in_specs=[in_place, in_place, in_vmem, in_vmem],
        out_specs=in_vmem,
        scratch_shapes=[
            pltpu.VMEM(block, F32),
            pltpu.VMEM(block, F32),
            pltpu.VMEM(block, F32),
            pltpu.VMEM((3,) + block, F32),
            pltpu.VMEM(block, F32),
            pltpu.VMEM(block, F32),
            pltpu.VMEM(block, F32),
            pltpu.VMEM(block, F32),
            pltpu.VMEM((2, 4, CHUNKS, LANES), F32),
            pltpu.VMEM((CHUNKS, LANES), jnp.int32),
            pltpu.VMEM((8, LANES), jnp.int32),
            pltpu.VMEM((4, CELLS, LANES), F32),
            pltpu.VMEM((FACTOR_PLANES, 8, LANES), F32),
            pltpu.VMEM((3, 2, CELLS, LANES), F32),
            pltpu.VMEM((3, 2, CELLS, LANES), F32),
            dma((6,)),
            dma((4,)),
            dma((6,)),
            dma((2,)),
            dma((2,)),
            dma((2,)),
            dma((3,)),
        ],
        compiler_params=pltpu.CompilerParams(collective_id=0, has_side_effects=True),
        name="line_implicit_step",
    )(view, rate, line_next.reshape(CHUNKS, LANES), face_codes)
    return state + update.transpose(0, 1, 3, 2, 4).reshape(state.shape)


def solution(mesh):
    placed = (P("inst", None, "cell", None), P("cell", None), P(), P())
    return jax.shard_map(
        local, mesh=mesh, in_specs=placed, out_specs=P("inst", None, "cell", None), check_vma=False
    )
```

profile of v0, /device:TPU:8, one launch (start us, length us, event | category | flops | bytes accessed | tf_op | source)
XLA Modules:
  0.0 47.2 jit_solution(4834742104327478321)
XLA Ops:
  0.0 0.0 copy-start
  0.0 45.5 %line_implicit_step.1 = f32[2,6,16,2,128]{4,3,2,1,0:T(2,128)} custom-call(f32[2,6,16,2,128]{4,3,2,1,0:T(2,128)} %bitcast.11, f32[16,2,128]{2,1,0:T(2,128)} %bitcast.12, s32[16,128]{1,0:T(8,128)} %bitcast.13, s32[2,64]{1,0:T(2,128)} %codes_ref.1), custom_call_target="tpu_custom_call" | custom-call | tf_op jit(solution)/shard_map/line_implicit_step/pallas_call | solution.py:486
  45.5 0.0 copy-done
  45.5 1.7 %bitcast_add_fusion = f32[2,6,2,2048]{3,2,1,0:T(2,128)} fusion(f32[2,6,2,2048]{3,2,1,0:T(2,128)S(1)} %copy-done, f32[2,6,16,2,128]{4,3,2,1,0:T(2,128)} %line_implicit_step.1), kind=kLoop, calls=%fused_computation | loop fusion | flops 49152 | bytes 589824 | tf_op jit(solution)/shard_map/add | solution.py:518
Async XLA Ops:
  0.0 45.5 %copy-start = (f32[2,6,2,2048]{3,2,1,0:T(2,128)S(1)}, f32[2,6,2,2048]{3,2,1,0:T(2,128)}, u32[]{:S(2)}) copy-start(f32[2,6,2,2048]{3,2,1,0:T(2,128)} %param.4) | copy-start | bytes 589828
where the time goes:
time: 47.3 us; the launch traced here: 47.2 us
  Pallas kernels  45.5 us (96%)
  other arithmetic  1.71 us (4%)
    pallas_call x1, Pallas kernels, local(): pl.pallas_call(kernel, out_shape=jax.ShapeDtypeStruct((2, 6, CHUNKS, 2, L...  45.5 us
    add x1, other arithmetic, local(): return state + update.transpose(0, 1, 3, 2, 4).reshape(state.shape)  1.71 us

commit v1 on v0

--- a/solution.py
+++ b/solution.py
@@ -266,22 +266,35 @@
     lax.fori_loop(0, CHUNKS, body, 0)
 
 
+def tell_depths(sem, me, depth, distance):
+    @pl.when(depth >= distance)
+    def _():
+        pl.semaphore_signal(sem, 1, device_id={"cell": me - 8 * distance})
+
+    @pl.when(depth < 8 - distance)
+    def _():
+        pl.semaphore_signal(sem, 1, device_id={"cell": me + 8 * distance})
+
+
+def depth_peers(depth, distance):
+    return jnp.where(depth >= distance, 1, 0) + jnp.where(depth < 8 - distance, 1, 0)
+
+
 def kernel(
     state_ref, rate_ref, next_ref, codes_ref, out_ref,
     own, low, high, other, shifted, kflux, kprev, rhs, lp, prev, codes, coef, fac, side, delta,
-    load_sem, ghost_sem, inst_sem, coef_sem, side_sem, back_sem, self_sem,
+    load_sem, ghost_sem, inst_sem, coef_sem, side_sem, back_sem, self_sem, known,
 ):
     me = lax.axis_index("cell")
     inst = lax.axis_index("inst")
     barrier = pltpu.get_barrier_semaphore()
 
-    def greet(j, carry):
-        pl.semaphore_signal(barrier, 1, device_id={"cell": lax.rem(me + j, CELLS)})
-        return carry
-
-    lax.fori_loop(1, CELLS, greet, 0)
+    depth = me >> 3
     for j in range(1, 4):
         pl.semaphore_signal(barrier, 1, device_id={"inst": inst ^ j})
+    for j in range(1, 5):
+        pl.semaphore_signal(barrier, 1, device_id={"cell": me ^ j})
+    tell_depths(barrier, me, depth, 1)
 
     loads = [
         pltpu.make_async_copy(state_ref.at[:, :, :, c], own.at[:, :, c], load_sem.at[c])
@@ -305,47 +318,6 @@
             lp[i, c] = jnp.abs(vel_x) + sound
         return carry
 
-    lax.fori_loop(0, 2, own_radius, 0)
-    gather_lines(own, shifted, next_ref)
-
-    pl.semaphore_wait(barrier, CELLS - 1 + 3)
-
-    right = lax.rem(me + 1, CELLS)
-    left = lax.rem(me + CELLS - 1, CELLS)
-    to_pair = pltpu.make_async_remote_copy(
-        own, other.at[1], inst_sem.at[0], inst_sem.at[1], device_id={"inst": inst ^ 2}
-    )
-    to_pair.start()
-    to_right = pltpu.make_async_remote_copy(
-        own, low, ghost_sem.at[0], ghost_sem.at[1], device_id={"cell": right}
-    )
-    to_right.start()
-    to_left = pltpu.make_async_remote_copy(
-        own, high, ghost_sem.at[2], ghost_sem.at[3], device_id={"cell": left}
-    )
-    to_left.start()
-    to_twin = pltpu.make_async_remote_copy(
-        own, other.at[0], inst_sem.at[2], inst_sem.at[3], device_id={"inst": inst ^ 1}
-    )
-    to_twin.start()
-
-    my_row = (me & 7) * 8 + (me >> 3)
-
-    def send_coef(j, carry):
-        peer = lax.rem(me + j, CELLS)
-        pltpu.make_async_remote_copy(
-            lp.at[peer >> 5, :, peer & 15],
-            coef.at[:, my_row],
-            coef_sem.at[0],
-            coef_sem.at[1],
-            device_id={"cell": peer},
-        ).start()
-        return carry
-
-    lax.fori_loop(1, CELLS, send_coef, 0)
-    my_coef = pltpu.make_async_copy(lp.at[me >> 5, :, me & 15], coef.at[:, my_row], self_sem.at[0])
-    my_coef.start()
-
     def pitch_flux(i, carry):
         for c in range(2):
             here = [own[i, v, c] for v in range(6)]
@@ -359,7 +331,59 @@
                 kflux[i, v, c] = 0.5 * (flux_h[v] + flux_t[v]) - radius * (there[v] - here[v])
         return carry
 
+    pl.semaphore_wait(barrier, 7 + depth_peers(depth, 1))
+    to_pair = pltpu.make_async_remote_copy(
+        own, other.at[1], inst_sem.at[0], inst_sem.at[1], device_id={"inst": inst ^ 2}
+    )
+    to_pair.start()
+    to_right = pltpu.make_async_remote_copy(
+        own, low, ghost_sem.at[0], ghost_sem.at[1], device_id={"cell": lax.rem(me + 1, CELLS)}
+    )
+    to_left = pltpu.make_async_remote_copy(
+        own, high, ghost_sem.at[2], ghost_sem.at[3], device_id={"cell": lax.rem(me + CELLS - 1, CELLS)}
+    )
+    row_start = (me & 3) == 0
+    row_end = (me & 3) == 3
+    first = me == 0
+    last = me == CELLS - 1
+    pl.when(jnp.logical_not(row_end))(to_right.start)
+    pl.when(jnp.logical_not(row_start))(to_left.start)
+    to_twin = pltpu.make_async_remote_copy(
+        own, other.at[0], inst_sem.at[2], inst_sem.at[3], device_id={"inst": inst ^ 1}
+    )
+    to_twin.start()
+
+    pl.semaphore_signal(known.at[0], 1, device_id={"cell": me ^ 4})
+    pl.semaphore_wait(known.at[0], 1)
+    tell_depths(known.at[1], me, depth, 1)
+    pl.semaphore_wait(known.at[1], depth_peers(depth, 1))
+    pl.when(jnp.logical_and(row_end, jnp.logical_not(last)))(to_right.start)
+    pl.when(jnp.logical_and(row_start, jnp.logical_not(first)))(to_left.start)
+    tell_depths(known.at[2], me, depth, 2)
+    lax.fori_loop(0, 2, own_radius, 0)
+    pl.semaphore_wait(known.at[2], depth_peers(depth, 2))
+    pl.semaphore_signal(known.at[3], 1, device_id={"cell": me ^ 32})
+    gather_lines(own, shifted, next_ref)
     lax.fori_loop(0, 2, pitch_flux, 0)
+    pl.semaphore_wait(known.at[3], 1)
+
+    my_row = (me & 7) * 8 + (me >> 3)
+
+    def send_coef(j, carry):
+        peer = lax.rem(me + j, CELLS)
+        pltpu.make_async_remote_copy(
+            lp.at[peer >> 5, :, peer & 15],
+            coef.at[:, my_row],
+            coef_sem.at[0],
+            coef_sem.at[1],
+            device_id={"cell": peer},
+        ).start()
+        return carry
+
+    lax.fori_loop(1, CELLS, send_coef, 0)
+    my_coef = pltpu.make_async_copy(lp.at[me >> 5, :, me & 15], coef.at[:, my_row], self_sem.at[0])
+    my_coef.start()
+
     gather_lines(kflux, kprev, prev)
 
     to_pair.wait_recv()
@@ -374,8 +398,8 @@
     my_coef.wait()
     factorise(coef, fac)
 
-    to_right.wait_recv()
-    to_left.wait_recv()
+    pl.when(jnp.logical_not(first))(to_right.wait_recv)
+    pl.when(jnp.logical_not(last))(to_left.wait_recv)
     spread = lax.broadcasted_iota(jnp.int32, (CHUNKS, LANES), 0) * 4 + (
         lax.broadcasted_iota(jnp.int32, (CHUNKS, LANES), 1) // TILE_LINES
     )
@@ -383,21 +407,29 @@
         jnp.take_along_axis(jnp.broadcast_to(codes[e : e + 1, :], (CHUNKS, LANES)), spread, axis=1)
         for e in range(2)
     ]
-    first = me == 0
-    last = me == CELLS - 1
+
+    @pl.when(first)
+    def _():
+        for i in range(2):
+            near, far = ghost_cells(
+                [own[i, v, 0] for v in range(6)], [own[i, v, 1] for v in range(6)], end_codes[0]
+            )
+            for v in range(6):
+                low[i, v, 0] = far[v]
+                low[i, v, 1] = near[v]
+
+    @pl.when(last)
+    def _():
+        for i in range(2):
+            near, far = ghost_cells(
+                [own[i, v, 1] for v in range(6)], [own[i, v, 0] for v in range(6)], end_codes[1]
+            )
+            for v in range(6):
+                high[i, v, 0] = near[v]
+                high[i, v, 1] = far[v]
 
     def add_line(i, carry):
-        mine = [[own[i, v, c] for v in range(6)] for c in range(2)]
-        low_near, low_far = ghost_cells(mine[0], mine[1], end_codes[0])
-        high_near, high_far = ghost_cells(mine[1], mine[0], end_codes[1])
-        cells = [
-            [jnp.where(first, low_far[v], low[i, v, 0]) for v in range(6)],
-            [jnp.where(first, low_near[v], low[i, v, 1]) for v in range(6)],
-            mine[0],
-            mine[1],
-            [jnp.where(last, high_near[v], high[i, v, 0]) for v in range(6)],
-            [jnp.where(last, high_far[v], high[i, v, 1]) for v in range(6)],
-        ]
+        cells = [[part[i, v, c] for v in range(6)] for part in (low, own, high) for c in range(2)]
         parts = line_part(cells)
         for c in range(2):
             for v in range(6):
@@ -466,8 +498,10 @@
         delta.at[:, :, my_row], out_ref.at[my_inst, pl.ds(my_var, 3), my_chunk], self_sem.at[2]
     )
     my_back.start()
-    for copy in (to_pair, to_right, to_left, to_twin, to_forward):
+    for copy in (to_pair, to_twin, to_forward):
         copy.wait_send()
+    pl.when(jnp.logical_not(last))(to_right.wait_send)
+    pl.when(jnp.logical_not(first))(to_left.wait_send)
     few = coef.at[:, pl.ds(0, CELLS - 1)]
     pltpu.make_async_copy(few, few, coef_sem.at[0]).wait()
     pltpu.make_async_copy(many, many, side_sem.at[0]).wait()
@@ -511,6 +545,7 @@
             dma((2,)),
             dma((2,)),
             dma((3,)),
+            pltpu.SemaphoreType.REGULAR((4,)),
         ],
         compiler_params=pltpu.CompilerParams(collective_id=0, has_side_effects=True),
         name="line_implicit_step",

time: 47.3 us -> 44.9 us (0.949); the launches traced: 47.2 us -> 44.1 us
  Pallas kernels: 45.5 us -> 42.4 us
    pallas_call x1, Pallas kernels: 45.5 us -> 42.4 us  [local(): pl.pallas_call(kernel, out_shape=jax.ShapeDtypeStruct((2, 6, CHUNKS, 2, L...]
where the time goes in v1:
time: 44.9 us; the launch traced here: 44.1 us
  Pallas kernels  42.4 us (94%)
  other arithmetic  1.71 us (4%)
    pallas_call x1, Pallas kernels, local(): pl.pallas_call(kernel, out_shape=jax.ShapeDtypeStruct((2, 6, CHUNKS, 2, L...  42.4 us
    add x1, other arithmetic, local(): return state + update.transpose(0, 1, 3, 2, 4).reshape(state.shape)  1.71 us

profile of v1, /device:TPU:8, one launch (start us, length us, event | category | flops | bytes accessed | tf_op | source)
XLA Modules:
  0.0 44.1 jit_solution(3304693031681889276)
XLA Ops:
  0.0 0.0 copy-start
  0.0 42.4 %line_implicit_step.1 = f32[2,6,16,2,128]{4,3,2,1,0:T(2,128)} custom-call(f32[2,6,16,2,128]{4,3,2,1,0:T(2,128)} %bitcast.11, f32[16,2,128]{2,1,0:T(2,128)} %bitcast.12, s32[16,128]{1,0:T(8,128)} %bitcast.13, s32[2,64]{1,0:T(2,128)} %codes_ref.1), custom_call_target="tpu_custom_call" | custom-call | tf_op jit(solution)/shard_map/line_implicit_step/pallas_call | solution.py:520
  42.4 0.0 copy-done
  42.4 1.7 %bitcast_add_fusion = f32[2,6,2,2048]{3,2,1,0:T(2,128)} fusion(f32[2,6,2,2048]{3,2,1,0:T(2,128)S(1)} %copy-done, f32[2,6,16,2,128]{4,3,2,1,0:T(2,128)} %line_implicit_step.1), kind=kLoop, calls=%fused_computation | loop fusion | flops 49152 | bytes 589824 | tf_op jit(solution)/shard_map/add | solution.py:553
Async XLA Ops:
  0.0 42.4 %copy-start = (f32[2,6,2,2048]{3,2,1,0:T(2,128)S(1)}, f32[2,6,2,2048]{3,2,1,0:T(2,128)}, u32[]{:S(2)}) copy-start(f32[2,6,2,2048]{3,2,1,0:T(2,128)} %param.4) | copy-start | bytes 589828

commit v2 on v1

v2 whole, which is shorter than its diff:
```python
import jax
import jax.numpy as jnp
import numpy as np
from jax import lax
from jax.experimental import pallas as pl
from jax.experimental.pallas import tpu as pltpu
from jax.sharding import PartitionSpec as P

NT = 8
CELLS = 64
CHUNKS = 16
LANES = 128
HALF = 64
TILE_LINES = 32
GAMMA_GAS = 1.4
FREE_STATE = (1.0, 0.5, 0.0, 0.0, 2.625, 0.2)
F32 = jnp.float32
FACTOR_PLANES = 84


def spectral_table():
    offsets = np.arange(NT)[:, None] - np.arange(NT)[None, :]
    angles = np.pi * offsets / NT
    safe_sin = np.where(offsets == 0, 1.0, np.sin(angles))
    parity = np.where(np.mod(offsets, 2) == 0, -1.0, 1.0)
    return np.where(offsets == 0, 0.0, 0.5 * parity * np.cos(angles) / safe_sin)


def time_weight(inst, row, slot, column):
    table = spectral_table()
    values = [float(table[2 * i + row, 2 * (i ^ slot) + column]) for i in range(NT // 2)]
    weight = jnp.float32(values[3])
    for i in (2, 1, 0):
        weight = jnp.where(inst == i, jnp.float32(values[i]), weight)
    return weight


def primitives(cell):
    inverse = 1.0 / cell[0]
    vel_x = cell[1] * inverse
    vel_y = cell[2] * inverse
    vel_z = cell[3] * inverse
    pressure = 0.4 * (cell[4] - 0.5 * cell[0] * (vel_x * vel_x + vel_y * vel_y + vel_z * vel_z))
    sound = jnp.sqrt(GAMMA_GAS * pressure * inverse)
    return vel_x, vel_y, pressure, sound


def flux(cell, velocity, pressure, component):
    rows = [cell[v] * velocity for v in range(6)]
    rows[component] = rows[component] + pressure
    rows[4] = rows[4] + pressure * velocity
    return rows


def swap(x):
    return pltpu.roll(x, HALF, x.ndim - 1)


def low_lanes(shape):
    return lax.broadcasted_iota(jnp.int32, shape, len(shape) - 1) < HALF


def pack(cell_a, cell_b):
    low = low_lanes(cell_a.shape)
    return jnp.where(low, cell_a, swap(cell_b)), jnp.where(low, swap(cell_a), cell_b)


def following(planes, swapped, p):
    low = low_lanes((8, LANES))
    return jnp.where(low, swapped[p], swapped[min(p + 1, len(planes) - 1)])


def preceding(planes, swapped, p):
    low = low_lanes((8, LANES))
    return jnp.where(low, swapped[max(p - 1, 0)], swapped[p])


def line_terms(state_ref, codes, line_ref):
    low = low_lanes((8, LANES))
    plane = lax.broadcasted_iota(jnp.int32, (8, LANES), 0)
    cells = []
    for v in range(6):
        inner = [state_ref[v, 8 * p : 8 * p + 8, :] for p in range(8)]
        ends = []
        for block, code, keep_low in ((inner[0], codes[0], True), (inner[7], codes[1], False)):
            turned = swap(block)
            mirror = -turned if v == 1 else turned
            copied = jnp.where(low, block, turned) if keep_low else jnp.where(low, turned, block)
            inflow = jnp.full((8, LANES), FREE_STATE[v], F32)
            ends.append(jnp.where(code == 0, mirror, jnp.where(code == 1, inflow, copied)))
        before = jnp.where(plane == 0, ends[0], pltpu.roll(inner[7], 1, 0))
        after = jnp.where(plane == 7, ends[1], pltpu.roll(inner[0], 7, 0))
        cells.append([before] + inner + [after])
    parts = [primitives([cells[v][p] for v in range(6)]) for p in range(10)]
    speed = [q[0] for q in parts]
    pressure = [q[2] for q in parts]
    radius = [jnp.abs(q[0]) + q[3] for q in parts]
    turned = [swap(q) for q in pressure]
    sensor = []
    for p in range(10):
        up, down = following(pressure, turned, p), preceding(pressure, turned, p)
        sensor.append(
            jnp.abs(up - 2.0 * pressure[p] + down) / (up + 2.0 * pressure[p] + down)
        )
    turned_sensor = [swap(q) for q in sensor]
    turned_radius = [swap(q) for q in radius]
    second, fourth, face_radius = [], [], []
    for p in range(9):
        e2 = 0.25 * jnp.maximum(sensor[p], following(sensor, turned_sensor, p))
        second.append(e2)
        fourth.append(jnp.maximum(0.0, 0.03125 - e2))
        face_radius.append(0.5 * (radius[p] + following(radius, turned_radius, p)))
    for v in range(6):
        own = cells[v]
        turned = [swap(q) for q in own]
        moved = [own[p] * speed[p] for p in range(10)]
        if v == 1:
            moved = [moved[p] + pressure[p] for p in range(10)]
        if v == 4:
            moved = [moved[p] + pressure[p] * speed[p] for p in range(10)]
        turned_moved = [swap(q) for q in moved]
        faces = []
        for p in range(9):
            near = following(own, turned, p) - own[p]
            far = own[p + 1] - preceding(own, turned, p) - 3.0 * near
            faces.append(
                0.5 * (moved[p] + following(moved, turned_moved, p))
                - face_radius[p] * (second[p] * near - fourth[p] * far)
            )
        turned_faces = [swap(q) for q in faces]
        for p in range(8):
            line_ref[v, 8 * p : 8 * p + 8, :] = faces[p + 1] - preceding(
                faces, turned_faces, p + 1
            )
    return radius


def mat_mat(a, b):
    return a[0] * b[0] + a[1] * swap(b[1]), a[0] * b[1] + a[1] * swap(b[0])


def mat_vec(a, x):
    return a[0] * x + a[1] * swap(x)


def mat_inv(m):
    turned = swap(m[0])
    reciprocal = 1.0 / (m[0] * turned - m[1] * swap(m[1]))
    return turned * reciprocal, -m[1] * reciprocal


def plus(a, b):
    return tuple(x + y for x, y in zip(a, b))


def minus(a):
    return tuple(-x for x in a)


def rolled(members, shift):
    return tuple(pltpu.roll(m, shift % 8, m.ndim - 2) for m in members)


STEPS = (
    (0, 1, 2, False),
    (2, 3, 4, False),
    (4, 5, 6, False),
    (6, 7, 0, True),
    (1, 3, 5, False),
    (5, 7, 1, True),
    (3, 7, 3, True),
)
BEFORE = {
    0: (7, True),
    2: (1, False),
    4: (3, False),
    6: (5, False),
    1: (7, True),
    5: (3, False),
    3: (7, True),
}
AFTER = {0: 1, 2: 3, 4: 5, 6: 7, 1: 3, 5: 7, 3: 7}


def factorise(radius, rate, fac_ref):
    low = low_lanes((8, LANES))
    plane = lax.broadcasted_iota(jnp.int32, (8, LANES), 0)
    radius = (
        [jnp.where(plane == 0, 0.0, radius[0])]
        + radius[1:9]
        + [jnp.where(plane == 7, 0.0, radius[9])]
    )
    turned = [swap(q) for q in radius]
    sub, diag, sup = {}, {}, {}
    for p in range(8):
        b = radius[p + 1]
        a = preceding(radius, turned, p + 1)
        c = following(radius, turned, p + 1)
        lower, upper = -(a + b), -(b + c)
        middle = rate[p] * b + 0.5 * (a + 2.0 * b + c) + 0.25 * (a + 4.0 * b + c)
        sub[p] = (0.25 * a, jnp.where(low, lower, 0.0))
        diag[p] = (middle, jnp.where(low, upper, lower))
        sup[p] = (0.25 * c, jnp.where(low, 0.0, upper))
    sub[0] = tuple(jnp.where(plane == 0, 0.0, m) for m in sub[0])
    sup[7] = tuple(jnp.where(plane == 7, 0.0, m) for m in sup[7])
    count = [0]

    def keep(members):
        for m in members:
            fac_ref[count[0]] = m
            count[0] += 1

    inverse = {}
    for e, o, n, wraps in STEPS:
        for x in (e, n):
            if x not in inverse:
                inverse[x] = mat_inv(diag[x])
        inv_n, sub_n, sup_n = inverse[n], sub[n], sup[n]
        if wraps:
            inv_n, sub_n, sup_n = rolled(inv_n, -1), rolled(sub_n, -1), rolled(sup_n, -1)
        left = minus(mat_mat(sub[o], inverse[e]))
        right = minus(mat_mat(sup[o], inv_n))
        keep(left)
        keep(right)
        keep(inverse[e])
        keep(mat_mat(inverse[e], sub[e]))
        keep(mat_mat(inverse[e], sup[e]))
        sub[o] = mat_mat(left, sub[e])
        diag[o] = plus(diag[o], plus(mat_mat(left, sup[e]), mat_mat(right, sub_n)))
        sup[o] = mat_mat(right, sup_n)
    s, d, u = sub[7], diag[7], sup[7]
    for h in (1, 2, 4):
        inv = mat_inv(d)
        left = minus(mat_mat(s, rolled(inv, h)))
        right = minus(mat_mat(u, rolled(inv, -h)))
        keep(left)
        keep(right)
        s_low, u_low = rolled(s, h), rolled(u, h)
        s_high, u_high = rolled(s, -h), rolled(u, -h)
        d = plus(d, plus(mat_mat(left, u_low), mat_mat(right, s_high)))
        s, u = mat_mat(left, s_low), mat_mat(right, u_high)
    keep(mat_inv(d))


def substitute(fac_ref, side_ref, line_ref, out_ref):
    def fac(first):
        return fac_ref[first][None], fac_ref[first + 1][None]

    def shift(x, count):
        return pltpu.roll(x, count % 8, 1)

    r = [side_ref[:, 8 * p : 8 * p + 8, :] - line_ref[:, 8 * p : 8 * p + 8, :] for p in range(8)]
    at = 0
    bases = {}
    for e, o, n, wraps in STEPS:
        side_n = shift(r[n], -1) if wraps else r[n]
        r[o] = r[o] + (mat_vec(fac(at), r[e]) + mat_vec(fac(at + 2), side_n))
        bases[e] = at + 4
        at += 10
    x = r[7]
    for h in (1, 2, 4):
        x = x + (mat_vec(fac(at), shift(x, h)) + mat_vec(fac(at + 2), shift(x, -h)))
        at += 4
    values = {7: mat_vec(fac(at), x)}
    for e in (3, 5, 1, 6, 4, 2, 0):
        base = bases[e]
        prior, wraps = BEFORE[e]
        low = shift(values[prior], 1) if wraps else values[prior]
        back = mat_vec(fac(base + 2), low) + mat_vec(fac(base + 4), values[AFTER[e]])
        values[e] = mat_vec(fac(base), r[e]) - back
    for p in range(8):
        out_ref[:, 8 * p : 8 * p + 8, :] = values[p]


def invert_lines(next_ref, prev_ref):
    lane = lax.broadcasted_iota(jnp.int32, (CHUNKS, LANES), 1).astype(F32)
    chunk = lax.broadcasted_iota(jnp.int32, (CHUNKS, LANES), 0)
    slot = lax.broadcasted_iota(jnp.int32, (LANES, LANES), 0)
    total = jnp.zeros((CHUNKS, LANES), F32)
    for q in range(CHUNKS):
        row = next_ref[q : q + 1, :]
        hit = jnp.broadcast_to(row >> 7, (CHUNKS, LANES)) == chunk
        place = jnp.where(jnp.broadcast_to(row & 127, (LANES, LANES)) == slot, 1.0, 0.0)
        left = jnp.concatenate([jnp.where(hit, lane, 0.0), jnp.where(hit, 1.0, 0.0)], axis=0)
        found = lax.dot_general(
            left.astype(jnp.bfloat16),
            place.astype(jnp.bfloat16),
            (((1,), (1,)), ((), ())),
            preferred_element_type=F32,
        )
        total = total + (found[:CHUNKS] + found[CHUNKS:] * (q * 128.0))
    prev_ref[...] = total.astype(jnp.int32)


def gather_lines(source, target, index_ref):
    source_rows = source.reshape(24 * CHUNKS, LANES)
    target_rows = target.reshape(24 * CHUNKS, LANES)

    def body(c, carry):
        row = jnp.broadcast_to(index_ref[pl.ds(c, 1), :], (8, LANES))
        lane = row & 127
        chunk = row >> 7
        found = [jnp.zeros((8, LANES), F32) for _ in range(3)]
        for s in range(CHUNKS):
            hit = chunk == s
            for g in range(3):
                rows = source_rows[pl.ds(g * 8 * CHUNKS + s, 8, stride=CHUNKS), :]
                found[g] = jnp.where(hit, jnp.take_along_axis(rows, lane, axis=1), found[g])
        for g in range(3):
            target_rows[pl.ds(g * 8 * CHUNKS + c, 8, stride=CHUNKS), :] = found[g]
        return carry

    lax.fori_loop(0, CHUNKS, body, 0)


def tell_depths(sem, me, depth, distance):
    @pl.when(depth >= distance)
    def _():
        pl.semaphore_signal(sem, 1, device_id={"cell": me - 8 * distance})

    @pl.when(depth < 8 - distance)
    def _():
        pl.semaphore_signal(sem, 1, device_id={"cell": me + 8 * distance})


def depth_peers(depth, distance):
    return jnp.where(depth >= distance, 1, 0) + jnp.where(depth < 8 - distance, 1, 0)


def kernel(
    state_ref, rate_ref, next_ref, codes_ref, out_ref,
    own, other, shifted, kflux, kprev, rate, sent_state, sent_side, prev, codes,
    lines, side, line, fac, delta, back,
    load_sem, inst_sem, state_sem, side_sem, back_sem, self_sem, known,
):
    me = lax.axis_index("cell")
    inst = lax.axis_index("inst")
    depth = me >> 3

    barrier = pltpu.get_barrier_semaphore()
    for j in range(1, 4):
        pl.semaphore_signal(barrier, 1, device_id={"inst": inst ^ j})
    for j in range(1, 5):
        pl.semaphore_signal(barrier, 1, device_id={"cell": me ^ j})
    tell_depths(barrier, me, depth, 1)
    loads = [
        pltpu.make_async_copy(state_ref.at[:, :, :, c], own.at[:, :, c], load_sem.at[c])
        for c in range(2)
    ] + [
        pltpu.make_async_copy(rate_ref.at[:, c], rate.at[c], load_sem.at[2 + c]) for c in range(2)
    ]
    for copy in loads:
        copy.start()
    pl.semaphore_wait(barrier, 7 + depth_peers(depth, 1))
    pl.semaphore_signal(known.at[0], 1, device_id={"cell": me ^ 4})
    for copy in loads:
        copy.wait()

    to_pair = [
        pltpu.make_async_remote_copy(
            own.at[i],
            other.at[1, i],
            inst_sem.at[0, i],
            inst_sem.at[1, i],
            device_id={"inst": inst ^ 2},
        )
        for i in range(2)
    ]
    to_twin = pltpu.make_async_remote_copy(
        own, other.at[0], inst_sem.at[2, 0], inst_sem.at[2, 1], device_id={"inst": inst ^ 1}
    )
    to_forward = [
        pltpu.make_async_remote_copy(
            other.at[1, i],
            other.at[2, i],
            inst_sem.at[3, i],
            inst_sem.at[4, i],
            device_id={"inst": inst ^ 1},
        )
        for i in range(2)
    ]
    for copy in to_pair:
        copy.start()
    to_twin.start()

    invert_lines(next_ref, prev)
    pl.semaphore_wait(known.at[0], 1)
    tell_depths(known.at[1], me, depth, 1)
    rate_rows = pack(rate[0], rate[1])

    def pack_state(i, carry):
        for v in range(6):
            rows = pack(own[i, v, 0], own[i, v, 1])
            for half in range(2):
                sent_state[i, half, v] = rows[half]
        for half in range(2):
            sent_state[i, half, 6] = rate_rows[half]
        return carry

    lax.fori_loop(0, 2, pack_state, 0)
    pl.semaphore_wait(known.at[1], depth_peers(depth, 1))
    tell_depths(known.at[2], me, depth, 2)
    gather_lines(own, shifted, next_ref)
    pl.semaphore_wait(known.at[2], depth_peers(depth, 2))
    pl.semaphore_signal(known.at[3], 1, device_id={"cell": me ^ 32})

    def pitch_flux(i, carry):
        for c in range(2):
            here = [own[i, v, c] for v in range(6)]
            there = [shifted[i, v, c] for v in range(6)]
            _, vel_h, p_h, sound_h = primitives(here)
            _, vel_t, p_t, sound_t = primitives(there)
            flux_h = flux(here, vel_h, p_h, 2)
            flux_t = flux(there, vel_t, p_t, 2)
            radius = 0.25 * (jnp.abs(vel_h) + sound_h + jnp.abs(vel_t) + sound_t)
            for v in range(6):
                kflux[i, v, c] = 0.5 * (flux_h[v] + flux_t[v]) - radius * (there[v] - here[v])
        return carry

    lax.fori_loop(0, 2, pitch_flux, 0)
    gather_lines(kflux, kprev, prev)
    pl.semaphore_wait(known.at[3], 1)

    my_row = (me & 7) * 8 + (me >> 3)
    my_inst, my_half, my_chunk = me >> 5, (me >> 4) & 1, me & 15

    def send_state(j, carry):
        peer = lax.rem(me + j, CELLS)
        pltpu.make_async_remote_copy(
            sent_state.at[peer >> 5, (peer >> 4) & 1, :, peer & 15],
            lines.at[:, my_row],
            state_sem.at[0],
            state_sem.at[1],
            device_id={"cell": peer},
        ).start()
        return carry

    lax.fori_loop(1, CELLS, send_state, 0)
    my_state = pltpu.make_async_copy(
        sent_state.at[my_inst, my_half, :, my_chunk], lines.at[:, my_row], self_sem.at[0]
    )
    my_state.start()

    weights = [
        [[time_weight(inst, n, slot, m) for m in range(2)] for slot in range(4)] for n in range(2)
    ]
    for i in range(2):
        to_pair[i].wait_recv()
        to_forward[i].start()
    to_twin.wait_recv()
    for copy in to_forward:
        copy.wait_recv()

    def add_time(v, carry):
        totals = [[None, None], [None, None]]
        for c in range(2):
            planes = [[own[m, v, c] for m in range(2)]] + [
                [other[slot, m, v, c] for m in range(2)] for slot in range(3)
            ]
            for n in range(2):
                total = kprev[n, v, c] - kflux[n, v, c]
                for slot in range(4):
                    for m in range(2):
                        if slot == 0 and m == n:
                            continue
                        total = total - weights[n][slot][m] * planes[slot][m]
                totals[n][c] = total
        for n in range(2):
            rows = pack(totals[n][0], totals[n][1])
            for half in range(2):
                sent_side[n, half, v] = rows[half]
        return carry

    lax.fori_loop(0, 6, add_time, 0)

    def send_side(j, carry):
        peer = lax.rem(me + j, CELLS)
        pltpu.make_async_remote_copy(
            sent_side.at[peer >> 5, (peer >> 4) & 1, :, peer & 15],
            side.at[:, my_row],
            side_sem.at[0],
            side_sem.at[1],
            device_id={"cell": peer},
        ).start()
        return carry

    lax.fori_loop(1, CELLS, send_side, 0)
    my_side = pltpu.make_async_copy(
        sent_side.at[my_inst, my_half, :, my_chunk], side.at[:, my_row], self_sem.at[1]
    )
    my_side.start()

    codes[...] = jnp.zeros((8, LANES), jnp.int32)
    codes[0:2, 0:64] = codes_ref[...]
    lane = lax.broadcasted_iota(jnp.int32, (8, LANES), 1)
    tile = my_chunk * 4 + my_half * 2 + ((lane & (HALF - 1)) >> 5)
    end_codes = [
        jnp.take_along_axis(jnp.broadcast_to(codes[e : e + 1, :], (8, LANES)), tile, axis=1)
        for e in range(2)
    ]
    many = lines.at[:, pl.ds(0, CELLS - 1)]
    pltpu.make_async_copy(many, many, state_sem.at[1]).wait()
    my_state.wait()
    radius = line_terms(lines, end_codes, line)
    factorise(radius, [lines[6, 8 * p : 8 * p + 8, :] for p in range(8)], fac)
    few = side.at[:, pl.ds(0, CELLS - 1)]
    pltpu.make_async_copy(few, few, side_sem.at[1]).wait()
    my_side.wait()
    substitute(fac, side, line, delta)

    def send_back(j, carry):
        peer = lax.rem(me + j, CELLS)
        pltpu.make_async_remote_copy(
            delta.at[:, (peer & 7) * 8 + (peer >> 3)],
            back.at[my_inst, my_half, :, my_chunk],
            back_sem.at[0],
            back_sem.at[1],
            device_id={"cell": peer},
        ).start()
        return carry

    lax.fori_loop(1, CELLS, send_back, 0)
    my_back = pltpu.make_async_copy(
        delta.at[:, my_row], back.at[my_inst, my_half, :, my_chunk], self_sem.at[2]
    )
    my_back.start()
    for copy in (*to_pair, to_twin, *to_forward):
        copy.wait_send()
    pltpu.make_async_copy(many, many, state_sem.at[0]).wait()
    pltpu.make_async_copy(few, few, side_sem.at[0]).wait()
    pltpu.make_async_copy(few, few, back_sem.at[0]).wait()
    pltpu.make_async_copy(few, few, back_sem.at[1]).wait()
    my_back.wait()

    def finish(i, carry):
        for v in range(6):
            update = pack(back[i, 0, v], back[i, 1, v])
            for c in range(2):
                out_ref[pl.ds((i * 6 + v) * 2 * CHUNKS + c, CHUNKS, stride=2), :] = (
                    own[i, v, c] + update[c]
                )
        return carry

    lax.fori_loop(0, 2, finish, 0)


def local(state, pseudo_rate, line_next, face_codes):
    view = state.reshape(2, 6, 2, CHUNKS, LANES).transpose(0, 1, 3, 2, 4)
    rate = pseudo_rate.reshape(2, CHUNKS, LANES).transpose(1, 0, 2)
    block = (2, 6, 2, CHUNKS, LANES)
    in_vmem = pl.BlockSpec(memory_space=pltpu.VMEM)
    in_place = pl.BlockSpec(memory_space=pl.ANY)
    dma = pltpu.SemaphoreType.DMA
    rows = pl.pallas_call(
        kernel,
        out_shape=jax.ShapeDtypeStruct((2 * 6 * CHUNKS * 2, LANES), F32),
        in_specs=[in_place, in_place, in_vmem, in_vmem],
        out_specs=in_vmem,
        scratch_shapes=[
            pltpu.VMEM(block, F32),
            pltpu.VMEM((3,) + block, F32),
            pltpu.VMEM(block, F32),
            pltpu.VMEM(block, F32),
            pltpu.VMEM(block, F32),
            pltpu.VMEM((2, CHUNKS, LANES), F32),
            pltpu.VMEM((2, 2, 7, CHUNKS, LANES), F32),
            pltpu.VMEM((2, 2, 6, CHUNKS, LANES), F32),
            pltpu.VMEM((CHUNKS, LANES), jnp.int32),
            pltpu.VMEM((8, LANES), jnp.int32),
            pltpu.VMEM((7, CELLS, LANES), F32),
            pltpu.VMEM((6, CELLS, LANES), F32),
            pltpu.VMEM((6, CELLS, LANES), F32),
            pltpu.VMEM((FACTOR_PLANES, 8, LANES), F32),
            pltpu.VMEM((6, CELLS, LANES), F32),
            pltpu.VMEM((2, 2, 6, CHUNKS, LANES), F32),
            dma((4,)),
            dma((5, 2)),
            dma((2,)),
            dma((2,)),
            dma((2,)),
            dma((3,)),
            pltpu.SemaphoreType.REGULAR((4,)),
        ],
        compiler_params=pltpu.CompilerParams(collective_id=0, has_side_effects=True),
        name="line_implicit_step",
    )(view, rate, line_next.reshape(CHUNKS, LANES), face_codes)
    return rows.reshape(2, 6, CHUNKS, 2, LANES).transpose(0, 1, 3, 2, 4).reshape(state.shape)


def solution(mesh):
    placed = (P("inst", None, "cell", None), P("cell", None), P(), P())
    return jax.shard_map(
        local, mesh=mesh, in_specs=placed, out_specs=P("inst", None, "cell", None), check_vma=False
    )
```

time: 44.9 us -> 42.8 us (0.953)
  Pallas kernels: 42.4 us -> 40.6 us
  other arithmetic: 1.71 us -> 0 us
  local copies, waits for them, and re-layouts: 0.01 us -> 1.62 us
    pallas_call x1, Pallas kernels: 42.4 us -> 40.6 us  [local(): pl.pallas_call(kernel, out_shape=jax.ShapeDtypeStruct((2 * 6 * CHUNKS * 2...]
    add x1 -> x0, other arithmetic: 1.71 us -> none  [local(): return state + update.transpose(0, 1, 3, 2, 4).reshape(state.shape)]
    unnamed x2 -> x1, local copies, waits for them, and re-layouts: 0.01 us -> 1.62 us
where the time goes in v2:
time: 42.8 us; the launch traced here: 42.2 us
  Pallas kernels  40.6 us (95%)
  local copies, waits for them, and re-layouts  1.62 us (4%)
    pallas_call x1, Pallas kernels, local(): pl.pallas_call(kernel, out_shape=jax.ShapeDtypeStruct((2 * 6 * CHUNKS * 2...  40.6 us
    unnamed x1, local copies, waits for them, and re-layouts  1.62 us

profile of v2, /device:TPU:8, one launch (start us, length us, event | category | flops | bytes accessed | tf_op | source)
XLA Modules:
  0.0 42.2 jit_solution(12194974641988753279)
XLA Ops:
  0.0 40.6 %line_implicit_step.1 = f32[384,128]{1,0:T(8,128)} custom-call(f32[2,6,16,2,128]{4,3,2,1,0:T(2,128)} %bitcast.13, f32[16,2,128]{2,1,0:T(2,128)} %bitcast.14, s32[16,128]{1,0:T(8,128)} %bitcast.15, s32[2,64]{1,0:T(2,128)} %codes_ref.1), custom_call_target="tpu_custom_call" | custom-call | tf_op jit(solution)/shard_map/line_implicit_step/pallas_call | solution.py:554
  40.6 1.6 %copy.7 = f32[2,6,2,2048]{3,2,1,0:T(2,128)} copy(f32[2,6,2,2048]{3,2,1,0:T(2,128)} %bitcast.12) | data formatting | bytes 393216

commit v3 on v2

--- a/solution.py
+++ b/solution.py
@@ -327,6 +327,17 @@
     return jnp.where(depth >= distance, 1, 0) + jnp.where(depth < 8 - distance, 1, 0)
 
 
+def farthest_first(me, send):
+    for steps in ((4,), (3, 5), (2, 6), (1, 7), (0,)):
+
+        def body(t, carry, steps=steps):
+            for step in steps:
+                send(lax.rem(me + 8 * step, CELLS) ^ (7 - t))
+            return carry
+
+        lax.fori_loop(0, 8 if steps[0] else 7, body, 0)
+
+
 def kernel(
     state_ref, rate_ref, next_ref, codes_ref, out_ref,
     own, other, shifted, kflux, kprev, rate, sent_state, sent_side, prev, codes,
@@ -424,8 +435,7 @@
     my_row = (me & 7) * 8 + (me >> 3)
     my_inst, my_half, my_chunk = me >> 5, (me >> 4) & 1, me & 15
 
-    def send_state(j, carry):
-        peer = lax.rem(me + j, CELLS)
+    def send_state(peer):
         pltpu.make_async_remote_copy(
             sent_state.at[peer >> 5, (peer >> 4) & 1, :, peer & 15],
             lines.at[:, my_row],
@@ -433,9 +443,8 @@
             state_sem.at[1],
             device_id={"cell": peer},
         ).start()
-        return carry
-
-    lax.fori_loop(1, CELLS, send_state, 0)
+
+    farthest_first(me, send_state)
     my_state = pltpu.make_async_copy(
         sent_state.at[my_inst, my_half, :, my_chunk], lines.at[:, my_row], self_sem.at[0]
     )
@@ -473,8 +482,7 @@
 
     lax.fori_loop(0, 6, add_time, 0)
 
-    def send_side(j, carry):
-        peer = lax.rem(me + j, CELLS)
+    def send_side(peer):
         pltpu.make_async_remote_copy(
             sent_side.at[peer >> 5, (peer >> 4) & 1, :, peer & 15],
             side.at[:, my_row],
@@ -482,9 +490,8 @@
             side_sem.at[1],
             device_id={"cell": peer},
         ).start()
-        return carry
-
-    lax.fori_loop(1, CELLS, send_side, 0)
+
+    farthest_first(me, send_side)
     my_side = pltpu.make_async_copy(
         sent_side.at[my_inst, my_half, :, my_chunk], side.at[:, my_row], self_sem.at[1]
     )
@@ -508,8 +515,7 @@
     my_side.wait()
     substitute(fac, side, line, delta)
 
-    def send_back(j, carry):
-        peer = lax.rem(me + j, CELLS)
+    def send_back(peer):
         pltpu.make_async_remote_copy(
             delta.at[:, (peer & 7) * 8 + (peer >> 3)],
             back.at[my_inst, my_half, :, my_chunk],
@@ -517,9 +523,8 @@
             back_sem.at[1],
             device_id={"cell": peer},
         ).start()
-        return carry
-
-    lax.fori_loop(1, CELLS, send_back, 0)
+
+    farthest_first(me, send_back)
     my_back = pltpu.make_async_copy(
         delta.at[:, my_row], back.at[my_inst, my_half, :, my_chunk], self_sem.at[2]
     )

time: 42.8 us -> 40.4 us (0.944)
  Pallas kernels: 40.6 us -> 38.5 us
    pallas_call x1, Pallas kernels: 40.6 us -> 38.5 us  [local(): pl.pallas_call(kernel, out_shape=jax.ShapeDtypeStruct((2 * 6 * CHUNKS * 2...]
where the time goes in v3:
time: 40.4 us; the launch traced here: 40.1 us
  Pallas kernels  38.5 us (95%)
  local copies, waits for them, and re-layouts  1.62 us (4%)
    pallas_call x1, Pallas kernels, local(): pl.pallas_call(kernel, out_shape=jax.ShapeDtypeStruct((2 * 6 * CHUNKS * 2...  38.5 us
    unnamed x1, local copies, waits for them, and re-layouts  1.62 us

profile of v3, /device:TPU:8, one launch (start us, length us, event | category | flops | bytes accessed | tf_op | source)
XLA Modules:
  0.0 40.1 jit_solution(11377642986250216355)
XLA Ops:
  0.0 38.5 %line_implicit_step.1 = f32[384,128]{1,0:T(8,128)} custom-call(f32[2,6,16,2,128]{4,3,2,1,0:T(2,128)} %bitcast.13, f32[16,2,128]{2,1,0:T(2,128)} %bitcast.14, s32[16,128]{1,0:T(8,128)} %bitcast.15, s32[2,64]{1,0:T(2,128)} %codes_ref.1), custom_call_target="tpu_custom_call" | custom-call | tf_op jit(solution)/shard_map/line_implicit_step/pallas_call | solution.py:559
  38.5 1.6 %copy.7 = f32[2,6,2,2048]{3,2,1,0:T(2,128)} copy(f32[2,6,2,2048]{3,2,1,0:T(2,128)} %bitcast.12) | data formatting | bytes 393216

commit v4 on v3

--- a/solution.py
+++ b/solution.py
@@ -313,26 +313,13 @@
     lax.fori_loop(0, CHUNKS, body, 0)
 
 
-def tell_depths(sem, me, depth, distance):
-    @pl.when(depth >= distance)
-    def _():
-        pl.semaphore_signal(sem, 1, device_id={"cell": me - 8 * distance})
-
-    @pl.when(depth < 8 - distance)
-    def _():
-        pl.semaphore_signal(sem, 1, device_id={"cell": me + 8 * distance})
-
-
-def depth_peers(depth, distance):
-    return jnp.where(depth >= distance, 1, 0) + jnp.where(depth < 8 - distance, 1, 0)
-
-
 def farthest_first(me, send):
     for steps in ((4,), (3, 5), (2, 6), (1, 7), (0,)):
-
-        def body(t, carry, steps=steps):
-            for step in steps:
-                send(lax.rem(me + 8 * step, CELLS) ^ (7 - t))
+        planes = [((me >> 3) + step) & 7 for step in steps]
+
+        def body(turn, carry, planes=planes):
+            for plane in planes:
+                send(plane, (me & 7) ^ (7 - turn))
             return carry
 
         lax.fori_loop(0, 8 if steps[0] else 7, body, 0)
@@ -351,9 +338,16 @@
     barrier = pltpu.get_barrier_semaphore()
     for j in range(1, 4):
         pl.semaphore_signal(barrier, 1, device_id={"inst": inst ^ j})
-    for j in range(1, 5):
-        pl.semaphore_signal(barrier, 1, device_id={"cell": me ^ j})
-    tell_depths(barrier, me, depth, 1)
+
+    @pl.when(depth < 7)
+    def _():
+        pl.semaphore_signal(barrier, 1, device_id={"cell": 56 + (me & 7)})
+
+    @pl.when(depth == 7)
+    def _():
+        for j in range(1, 5):
+            pl.semaphore_signal(barrier, 1, device_id={"cell": me ^ j})
+
     loads = [
         pltpu.make_async_copy(state_ref.at[:, :, :, c], own.at[:, :, c], load_sem.at[c])
         for c in range(2)
@@ -362,8 +356,13 @@
     ]
     for copy in loads:
         copy.start()
-    pl.semaphore_wait(barrier, 7 + depth_peers(depth, 1))
-    pl.semaphore_signal(known.at[0], 1, device_id={"cell": me ^ 4})
+    pl.semaphore_wait(barrier, jnp.where(depth == 7, 14, 3))
+
+    @pl.when(depth == 7)
+    def _():
+        for j in range(1, 4):
+            pl.semaphore_signal(known.at[0], 1, device_id={"cell": me ^ j})
+
     for copy in loads:
         copy.wait()
 
@@ -394,9 +393,12 @@
         copy.start()
     to_twin.start()
 
+    @pl.when(depth == 7)
+    def _():
+        pl.semaphore_wait(known.at[0], 3)
+        pl.semaphore_signal(known.at[1], 1, device_id={"cell": me ^ 4})
+
     invert_lines(next_ref, prev)
-    pl.semaphore_wait(known.at[0], 1)
-    tell_depths(known.at[1], me, depth, 1)
     rate_rows = pack(rate[0], rate[1])
 
     def pack_state(i, carry):
@@ -409,11 +411,14 @@
         return carry
 
     lax.fori_loop(0, 2, pack_state, 0)
-    pl.semaphore_wait(known.at[1], depth_peers(depth, 1))
-    tell_depths(known.at[2], me, depth, 2)
+
+    @pl.when(depth == 7)
+    def _():
+        pl.semaphore_wait(known.at[1], 1)
+        for j in (4, 5, 3, 6, 2, 7, 1):
+            pl.semaphore_signal(known.at[2], 1, device_id={"cell": me - 8 * j})
+
     gather_lines(own, shifted, next_ref)
-    pl.semaphore_wait(known.at[2], depth_peers(depth, 2))
-    pl.semaphore_signal(known.at[3], 1, device_id={"cell": me ^ 32})
 
     def pitch_flux(i, carry):
         for c in range(2):
@@ -430,18 +435,25 @@
 
     lax.fori_loop(0, 2, pitch_flux, 0)
     gather_lines(kflux, kprev, prev)
-    pl.semaphore_wait(known.at[3], 1)
+    for i in range(2):
+        to_pair[i].wait_recv()
+        to_forward[i].start()
+
+    @pl.when(depth < 7)
+    def _():
+        pl.semaphore_wait(known.at[2], 1)
+
 
     my_row = (me & 7) * 8 + (me >> 3)
     my_inst, my_half, my_chunk = me >> 5, (me >> 4) & 1, me & 15
 
-    def send_state(peer):
+    def send_state(plane, place):
         pltpu.make_async_remote_copy(
-            sent_state.at[peer >> 5, (peer >> 4) & 1, :, peer & 15],
+            sent_state.at[plane >> 2, (plane >> 1) & 1, :, (plane & 1) * 8 + place],
             lines.at[:, my_row],
             state_sem.at[0],
             state_sem.at[1],
-            device_id={"cell": peer},
+            device_id={"cell": plane * 8 + place},
         ).start()
 
     farthest_first(me, send_state)
@@ -453,9 +465,6 @@
     weights = [
         [[time_weight(inst, n, slot, m) for m in range(2)] for slot in range(4)] for n in range(2)
     ]
-    for i in range(2):
-        to_pair[i].wait_recv()
-        to_forward[i].start()
     to_twin.wait_recv()
     for copy in to_forward:
         copy.wait_recv()
@@ -482,13 +491,13 @@
 
     lax.fori_loop(0, 6, add_time, 0)
 
-    def send_side(peer):
+    def send_side(plane, place):
         pltpu.make_async_remote_copy(
-            sent_side.at[peer >> 5, (peer >> 4) & 1, :, peer & 15],
+            sent_side.at[plane >> 2, (plane >> 1) & 1, :, (plane & 1) * 8 + place],
             side.at[:, my_row],
             side_sem.at[0],
             side_sem.at[1],
-            device_id={"cell": peer},
+            device_id={"cell": plane * 8 + place},
         ).start()
 
     farthest_first(me, send_side)
@@ -515,13 +524,13 @@
     my_side.wait()
     substitute(fac, side, line, delta)
 
-    def send_back(peer):
+    def send_back(plane, place):
         pltpu.make_async_remote_copy(
-            delta.at[:, (peer & 7) * 8 + (peer >> 3)],
+            delta.at[:, place * 8 + plane],
             back.at[my_inst, my_half, :, my_chunk],
             back_sem.at[0],
             back_sem.at[1],
-            device_id={"cell": peer},
+            device_id={"cell": plane * 8 + place},
         ).start()
 
     farthest_first(me, send_back)
@@ -584,7 +593,7 @@
             dma((2,)),
             dma((2,)),
             dma((3,)),
-            pltpu.SemaphoreType.REGULAR((4,)),
+            pltpu.SemaphoreType.REGULAR((3,)),
         ],
         compiler_params=pltpu.CompilerParams(collective_id=0, has_side_effects=True),
         name="line_implicit_step",

time: 40.4 us -> 39.2 us (0.970)
  Pallas kernels: 38.5 us -> 37.4 us
    pallas_call x1, Pallas kernels: 38.5 us -> 37.4 us  [local(): pl.pallas_call(kernel, out_shape=jax.ShapeDtypeStruct((2 * 6 * CHUNKS * 2...]
where the time goes in v4:
time: 39.2 us; the launch traced here: 39.1 us
  Pallas kernels  37.4 us (95%)
  local copies, waits for them, and re-layouts  1.62 us (4%)
    pallas_call x1, Pallas kernels, local(): pl.pallas_call(kernel, out_shape=jax.ShapeDtypeStruct((2 * 6 * CHUNKS * 2...  37.4 us
    unnamed x1, local copies, waits for them, and re-layouts  1.62 us

profile of v4, /device:TPU:8, one launch (start us, length us, event | category | flops | bytes accessed | tf_op | source)
XLA Modules:
  0.0 39.1 jit_solution(15332696307262654798)
XLA Ops:
  0.0 37.4 %line_implicit_step.1 = f32[384,128]{1,0:T(8,128)} custom-call(f32[2,6,16,2,128]{4,3,2,1,0:T(2,128)} %bitcast.13, f32[16,2,128]{2,1,0:T(2,128)} %bitcast.14, s32[16,128]{1,0:T(8,128)} %bitcast.15, s32[2,64]{1,0:T(2,128)} %codes_ref.1), custom_call_target="tpu_custom_call" | custom-call | tf_op jit(solution)/shard_map/line_implicit_step/pallas_call | solution.py:568
  37.5 1.6 %copy.7 = f32[2,6,2,2048]{3,2,1,0:T(2,128)} copy(f32[2,6,2,2048]{3,2,1,0:T(2,128)} %bitcast.12) | data formatting | bytes 393216

commit v5 on v4

--- a/solution.py
+++ b/solution.py
@@ -418,6 +418,19 @@
         for j in (4, 5, 3, 6, 2, 7, 1):
             pl.semaphore_signal(known.at[2], 1, device_id={"cell": me - 8 * j})
 
+    my_row = (me & 7) * 8 + (me >> 3)
+    my_inst, my_half, my_chunk = me >> 5, (me >> 4) & 1, me & 15
+
+    def send_state(plane, place):
+        pltpu.make_async_remote_copy(
+            sent_state.at[plane >> 2, (plane >> 1) & 1, :, (plane & 1) * 8 + place],
+            lines.at[:, my_row],
+            state_sem.at[0],
+            state_sem.at[1],
+            device_id={"cell": plane * 8 + place},
+        ).start()
+
+    pl.when(depth == 7)(lambda: farthest_first(me, send_state))
     gather_lines(own, shifted, next_ref)
 
     def pitch_flux(i, carry):
@@ -444,19 +457,7 @@
         pl.semaphore_wait(known.at[2], 1)
 
 
-    my_row = (me & 7) * 8 + (me >> 3)
-    my_inst, my_half, my_chunk = me >> 5, (me >> 4) & 1, me & 15
-
-    def send_state(plane, place):
-        pltpu.make_async_remote_copy(
-            sent_state.at[plane >> 2, (plane >> 1) & 1, :, (plane & 1) * 8 + place],
-            lines.at[:, my_row],
-            state_sem.at[0],
-            state_sem.at[1],
-            device_id={"cell": plane * 8 + place},
-        ).start()
-
-    farthest_first(me, send_state)
+    pl.when(depth < 7)(lambda: farthest_first(me, send_state))
     my_state = pltpu.make_async_copy(
         sent_state.at[my_inst, my_half, :, my_chunk], lines.at[:, my_row], self_sem.at[0]
     )
@@ -556,6 +557,10 @@
         return carry
 
     lax.fori_loop(0, 2, finish, 0)
+
+
+def hand_over(rows_ref, out_ref):
+    out_ref[...] = rows_ref[...]
 
 
 def local(state, pseudo_rate, line_next, face_codes):
@@ -598,6 +603,13 @@
         compiler_params=pltpu.CompilerParams(collective_id=0, has_side_effects=True),
         name="line_implicit_step",
     )(view, rate, line_next.reshape(CHUNKS, LANES), face_codes)
+    rows = pl.pallas_call(
+        hand_over,
+        out_shape=jax.ShapeDtypeStruct(rows.shape, F32),
+        in_specs=[in_vmem],
+        out_specs=in_vmem,
+        name="hand_over",
+    )(rows)
     return rows.reshape(2, 6, CHUNKS, 2, LANES).transpose(0, 1, 3, 2, 4).reshape(state.shape)
 
 

time: 39.2 us -> 38.4 us (0.980)
  local copies, waits for them, and re-layouts: 1.62 us -> 0 us
  Pallas kernels: 37.4 us -> 38.3 us
    pallas_call x0 -> x1, Pallas kernels: none -> 1.62 us  [local(): pl.pallas_call(hand_over, out_shape=jax.ShapeDtypeStruct(rows.shape, F32)...]
    unnamed x1 -> x0, local copies, waits for them, and re-layouts: 1.62 us -> none
    pallas_call x1, Pallas kernels: 37.4 us -> 36.6 us  [local(): pl.pallas_call(kernel, out_shape=jax.ShapeDtypeStruct((2 * 6 * CHUNKS * 2...]
where the time goes in v5:
time: 38.4 us; the launch traced here: 38.3 us
  Pallas kernels  38.3 us (100%)
    pallas_call x1, Pallas kernels, local(): pl.pallas_call(kernel, out_shape=jax.ShapeDtypeStruct((2 * 6 * CHUNKS * 2...  36.6 us
    pallas_call x1, Pallas kernels, local(): pl.pallas_call(hand_over, out_shape=jax.ShapeDtypeStruct(rows.shape, F32)...  1.62 us

profile of v5, /device:TPU:8, one launch (start us, length us, event | category | flops | bytes accessed | tf_op | source)
XLA Modules:
  0.0 38.3 jit_solution(6325450379964267029)
XLA Ops:
  0.0 36.6 %line_implicit_step.1.rows_ref = f32[384,128]{1,0:T(8,128)} custom-call(f32[2,6,16,2,128]{4,3,2,1,0:T(2,128)} %bitcast.12, f32[16,2,128]{2,1,0:T(2,128)} %bitcast.13, s32[16,128]{1,0:T(8,128)} %bitcast.14, s32[2,64]{1,0:T(2,128)} %codes_ref.1), custom_call_target="tpu_custom_call" | custom-call | tf_op jit(solution)/shard_map/line_implicit_step/pallas_call | solution.py:573
  36.6 1.6 %hand_over.1 = f32[384,128]{1,0:T(8,128)} custom-call(f32[384,128]{1,0:T(8,128)} %line_implicit_step.1.rows_ref), custom_call_target="tpu_custom_call" | custom-call | tf_op jit(solution)/shard_map/hand_over/pallas_call | solution.py:606

commit v6 on v5

--- a/solution.py
+++ b/solution.py
@@ -292,9 +292,11 @@
     prev_ref[...] = total.astype(jnp.int32)
 
 
-def gather_lines(source, target, index_ref):
+def gather_lines(source, target, index_ref, turned):
     source_rows = source.reshape(24 * CHUNKS, LANES)
     target_rows = target.reshape(24 * CHUNKS, LANES)
+    for s in range(CHUNKS):
+        turned[s] = source_rows[pl.ds(s, 24, stride=CHUNKS), :]
 
     def body(c, carry):
         row = jnp.broadcast_to(index_ref[pl.ds(c, 1), :], (8, LANES))
@@ -304,7 +306,7 @@
         for s in range(CHUNKS):
             hit = chunk == s
             for g in range(3):
-                rows = source_rows[pl.ds(g * 8 * CHUNKS + s, 8, stride=CHUNKS), :]
+                rows = turned[s, 8 * g : 8 * g + 8, :]
                 found[g] = jnp.where(hit, jnp.take_along_axis(rows, lane, axis=1), found[g])
         for g in range(3):
             target_rows[pl.ds(g * 8 * CHUNKS + c, 8, stride=CHUNKS), :] = found[g]
@@ -327,7 +329,7 @@
 
 def kernel(
     state_ref, rate_ref, next_ref, codes_ref, out_ref,
-    own, other, shifted, kflux, kprev, rate, sent_state, sent_side, prev, codes,
+    own, other, turned, shifted, kflux, kprev, rate, sent_state, sent_side, prev, codes,
     lines, side, line, fac, delta, back,
     load_sem, inst_sem, state_sem, side_sem, back_sem, self_sem, known,
 ):
@@ -431,7 +433,7 @@
         ).start()
 
     pl.when(depth == 7)(lambda: farthest_first(me, send_state))
-    gather_lines(own, shifted, next_ref)
+    gather_lines(own, shifted, next_ref, turned)
 
     def pitch_flux(i, carry):
         for c in range(2):
@@ -447,7 +449,7 @@
         return carry
 
     lax.fori_loop(0, 2, pitch_flux, 0)
-    gather_lines(kflux, kprev, prev)
+    gather_lines(kflux, kprev, prev, turned)
     for i in range(2):
         to_pair[i].wait_recv()
         to_forward[i].start()
@@ -578,6 +580,7 @@
         scratch_shapes=[
             pltpu.VMEM(block, F32),
             pltpu.VMEM((3,) + block, F32),
+            pltpu.VMEM((CHUNKS, 24, LANES), F32),
             pltpu.VMEM(block, F32),
             pltpu.VMEM(block, F32),
             pltpu.VMEM(block, F32),

time: 38.4 us -> 38.5 us (level)
  no operation moved by 1% of the time
where the time goes in v6:
time: 38.5 us; the launch traced here: 38.3 us
  Pallas kernels  38.3 us (99%)
    pallas_call x1, Pallas kernels, local(): pl.pallas_call(kernel, out_shape=jax.ShapeDtypeStruct((2 * 6 * CHUNKS * 2...  36.7 us
    pallas_call x1, Pallas kernels, local(): pl.pallas_call(hand_over, out_shape=jax.ShapeDtypeStruct(rows.shape, F32)...  1.62 us

profile of v6, /device:TPU:8, one launch (start us, length us, event | category | flops | bytes accessed | tf_op | source)
XLA Modules:
  0.0 38.3 jit_solution(5390045349653728944)
XLA Ops:
  0.0 36.7 %line_implicit_step.1.rows_ref = f32[384,128]{1,0:T(8,128)} custom-call(f32[2,6,16,2,128]{4,3,2,1,0:T(2,128)} %bitcast.12, f32[16,2,128]{2,1,0:T(2,128)} %bitcast.13, s32[16,128]{1,0:T(8,128)} %bitcast.14, s32[2,64]{1,0:T(2,128)} %codes_ref.1), custom_call_target="tpu_custom_call" | custom-call | tf_op jit(solution)/shard_map/line_implicit_step/pallas_call | solution.py:575
  36.7 1.6 %hand_over.1 = f32[384,128]{1,0:T(8,128)} custom-call(f32[384,128]{1,0:T(8,128)} %line_implicit_step.1.rows_ref), custom_call_target="tpu_custom_call" | custom-call | tf_op jit(solution)/shard_map/hand_over/pallas_call | solution.py:609
